TPU v7x, 32 devices: a whole 2x2x4 slice. The times are simulated.
32 devices in a mesh: fiber: 8 (over z, x), seg: 4 (over y, core).
Axes of the slice: x: 2, y: 2, z: 4, core: 2. Of those that a mesh axis runs over, the one named last changes fastest.
Arguments:
- raw_strain: bfloat16 [64, 1024, 2048], P('seg', 'fiber'), may hold values from -6 to 6
- fir_taps: float32 [31], replicated, may hold values from -1 to 1
- good_mask: int32 [64, 1024], P('seg', 'fiber'), may hold values from 0 to 1, as said below
Outputs:
- stacked_spectra: float32 [144, 1024, 2, 128], P('seg', 'fiber')
Inputs may be any that keep to these rules, and one draw needn't show every extreme that they name: `good_mask`: 0 or 1; some channels are 0 in every segment.
All inputs are finite; a program needn't handle non-finite values.
Results may differ from a plain program's by a relative error of at most 0.005.
Values may be sent and summed in bfloat16 or wider, within the bound.
A program may use at most 192 MiB of HBM per device.

v0:
```python
import functools
import math

import jax
import jax.numpy as jnp
import numpy as np
from jax import lax
from jax.experimental import pallas as pl
from jax.experimental.pallas import tpu as pltpu
from jax.sharding import PartitionSpec as P

NF = 144
LOW = 16
SMOOTH = 4
LAGS = 128
EDGE = 16

epsilon = 1e-06
water_share = 0.1
MESH = pl.DeviceIdType.MESH


def row_bins(shares):
    per = NF // shares
    return np.concatenate([np.tile(np.arange(k * per, (k + 1) * per), 2) for k in range(shares)])


def row_parts(shares):
    per = NF // shares
    return np.tile(np.repeat(np.arange(2), per), shares)


def dft_rows(samples, shares):
    bins, parts = row_bins(shares), row_parts(shares)
    index = ((bins[:, None] + LOW) * np.arange(samples)[None, :]) % samples
    angles = index.astype(np.float64) * (2.0 * math.pi / samples)
    return np.where(parts[:, None] == 0, np.cos(angles), -np.sin(angles)).astype(jnp.bfloat16)


def smooth_rows(shares):
    bins = row_bins(shares)
    return (np.abs(bins[:, None] - bins[None, :]) <= SMOOTH).astype(jnp.bfloat16)


def two_terms(x):
    hi = x.astype(jnp.bfloat16)
    return hi, (x - hi.astype(jnp.float32)).astype(jnp.bfloat16)


def mm(a, b):
    return jnp.dot(a, b, preferred_element_type=jnp.float32)


def mm_t(a, b):
    return lax.dot_general(a, b, (((1,), (1,)), ((), ())), preferred_element_type=jnp.float32)


def spectra_kernel(
    fibers, shares, taps_ref, raw_ref, mask_ref, basis_ref, smooth_ref,
    own_ref, next_ref,
    raw_v, edge_v, spec_v, out_l, out_r, in_l, in_r, band_v, mask_v, white_v, send_v,
    raw_sem, edge_sem, halo_send, halo_recv, send_sem, recv_sem, local_sem,
):
    fib = lax.axis_index("fiber")
    seg = lax.axis_index("seg")
    segs, channels, _ = raw_ref.shape
    rows = basis_ref.shape[0]
    per = rows // shares
    taps = taps_ref.shape[0]
    half = (taps - 1) // 2
    has_prev = fib > 0
    has_next = fib < fibers - 1

    edge_copies = [
        pltpu.make_async_copy(raw_ref.at[:, pl.ds(start, EDGE), :], edge_v.at[i], edge_sem.at[i])
        for i, start in enumerate((0, channels - EDGE))
    ]
    for copy in edge_copies:
        copy.start()
    pairs = segs // 2
    raw_copies = [
        pltpu.make_async_copy(raw_ref.at[pl.ds(2 * p, 2)], raw_v.at[p], raw_sem.at[p])
        for p in range(pairs)
    ]
    for copy in raw_copies:
        copy.start()

    barrier = pltpu.get_barrier_semaphore()
    for d in range(1, shares):
        pl.semaphore_signal(
            barrier, inc=1, device_id=(fib, lax.rem(seg + d, shares)), device_id_type=MESH
        )
    @pl.when(has_prev)
    def _():
        for k in range(shares):
            pl.semaphore_signal(barrier, inc=1, device_id=(fib - 1, k), device_id_type=MESH)
    @pl.when(has_next)
    def _():
        for k in range(shares):
            pl.semaphore_signal(barrier, inc=1, device_id=(fib + 1, k), device_id_type=MESH)

    row = lax.broadcasted_iota(jnp.int32, (2 * channels, channels), 0)
    col = lax.broadcasted_iota(jnp.int32, (2 * channels, channels), 1)
    left = row - channels - EDGE
    right = row - EDGE
    place = jnp.where(row < channels, row, jnp.where(left < 0, left, right))
    place = jnp.where(row < channels + 2 * EDGE, place, 8 * channels)
    tap = place - col + half
    band = jnp.zeros((2 * channels, channels), jnp.float32)
    for j in range(taps):
        band = jnp.where(tap == j, taps_ref[j], band)
    band_hi, band_lo = two_terms(band)
    band_v[:, :channels] = band_hi
    band_v[:, channels:] = band_lo
    mask_v[...] = mask_ref[...].astype(jnp.float32)
    for k in range(shares):
        send_v[k, per] = mask_ref[...].astype(jnp.float32).astype(jnp.bfloat16)

    @pl.when(jnp.logical_not(has_prev))
    def _():
        in_l[...] = jnp.zeros_like(in_l)
    @pl.when(jnp.logical_not(has_next))
    def _():
        in_r[...] = jnp.zeros_like(in_r)
        next_ref[...] = jnp.zeros_like(next_ref)

    edge_copies[0].wait()
    out_l[...] = mm_t(basis_ref[...], edge_v[0].reshape(segs * EDGE, -1))
    edge_copies[1].wait()
    out_r[...] = mm_t(basis_ref[...], edge_v[1].reshape(segs * EDGE, -1))

    sides = (fib + fibers - 1) // fibers + (2 * fibers - 2 - fib) // fibers
    pl.semaphore_wait(barrier, shares - 1 + shares * sides)

    to_prev = pltpu.make_async_remote_copy(
        src_ref=out_l, dst_ref=in_r, send_sem=halo_send.at[0], recv_sem=halo_recv.at[0],
        device_id=(jnp.maximum(fib - 1, 0), seg), device_id_type=MESH,
    )
    to_next = pltpu.make_async_remote_copy(
        src_ref=out_r, dst_ref=in_l, send_sem=halo_send.at[1], recv_sem=halo_recv.at[1],
        device_id=(jnp.minimum(fib + 1, fibers - 1), seg), device_id_type=MESH,
    )
    @pl.when(has_prev)
    def _():
        to_prev.start()
    @pl.when(has_next)
    def _():
        to_next.start()

    for p in range(pairs):
        raw_copies[p].wait()
        spec_v[p] = mm_t(basis_ref[...], raw_v[p].reshape(2 * channels, -1))

    @pl.when(has_prev)
    def _():
        to_next.wait_recv()
    @pl.when(has_next)
    def _():
        to_prev.wait_recv()

    per_tile = channels // EDGE
    lane = lax.broadcasted_iota(jnp.int32, (rows, channels), 1)

    def whiten_pair(p, carry):
        group = (2 * p) // per_tile
        base = pl.multiple_of(group * channels, channels)
        lefts = in_l[:, pl.ds(base, channels)]
        rights = in_r[:, pl.ds(base, channels)]
        parts = []
        for h in range(2):
            slot = lax.rem(2 * p + h, per_tile)
            l_roll = lax.rem(channels - slot * EDGE, channels)
            r_roll = lax.rem(channels + EDGE - slot * EDGE, channels)
            edges = jnp.where(
                lane < EDGE, pltpu.roll(lefts, l_roll, 1), pltpu.roll(rights, r_roll, 1)
            )
            both = jnp.concatenate([spec_v[p, :, h * channels : (h + 1) * channels], edges], axis=1)
            hi, lo = two_terms(both)
            wide = mm(hi, band_v[...])
            parts.append(
                wide[:, :channels] + wide[:, channels:] + mm(lo, band_v[:, :channels])
            )
        filtered = jnp.concatenate(parts, axis=1)
        power = filtered * filtered
        hi, lo = two_terms(power)
        smooth = mm(smooth_ref[...], hi) + mm(smooth_ref[...], lo)
        total = jnp.sum(power, axis=0, keepdims=True)
        level = smooth * (1.0 / (2 * SMOOTH + 1)) + (total * (water_share / NF) + epsilon)
        good = jnp.concatenate([mask_v[pl.ds(2 * p, 1), :], mask_v[pl.ds(2 * p + 1, 1), :]], axis=1)
        white = filtered * (lax.rsqrt(level) * good)
        white_v[pl.ds(2 * p, rows, segs), :] = white[:, :channels]
        white_v[pl.ds(2 * p + 1, rows, segs), :] = white[:, channels:]
        return carry

    lax.fori_loop(0, pairs, whiten_pair, 0)

    prev = jnp.maximum(fib - 1, 0)
    later = []
    own = []
    for k in range(shares):
        send_v[k, :per] = (
            white_v[k * per * segs : (k + 1) * per * segs, :]
            .reshape(per, segs, channels)
            .astype(jnp.bfloat16)
        )
        later.append(
            pltpu.make_async_remote_copy(
                src_ref=send_v.at[k], dst_ref=next_ref.at[seg],
                send_sem=send_sem.at[k], recv_sem=recv_sem.at[seg],
                device_id=(prev, k), device_id_type=MESH,
            )
        )
        @pl.when(has_prev)
        def _():
            later[k].start()
    for d in range(1, shares):
        other = lax.rem(seg + d, shares)
        own.append(
            pltpu.make_async_remote_copy(
                src_ref=send_v.at[other], dst_ref=own_ref.at[seg],
                send_sem=send_sem.at[shares + d], recv_sem=recv_sem.at[shares + seg],
                device_id=(fib, other), device_id_type=MESH,
            )
        )
        own[-1].start()
    mine = pltpu.make_async_copy(send_v.at[seg], own_ref.at[seg], local_sem.at[0])
    mine.start()
    mine.wait()
    for d in range(1, shares):
        source = lax.rem(seg + d, shares)
        pltpu.make_async_remote_copy(
            src_ref=send_v.at[source], dst_ref=own_ref.at[source],
            send_sem=send_sem.at[shares + d], recv_sem=recv_sem.at[shares + source],
            device_id=(fib, source), device_id_type=MESH,
        ).wait_recv()
    @pl.when(has_next)
    def _():
        for k in range(shares):
            pltpu.make_async_remote_copy(
                src_ref=send_v.at[k], dst_ref=next_ref.at[k],
                send_sem=send_sem.at[k], recv_sem=recv_sem.at[k],
                device_id=(prev, k), device_id_type=MESH,
            ).wait_recv()
    for copy in own:
        copy.wait_send()
    @pl.when(has_prev)
    def _():
        for copy in later:
            copy.wait_send()
        to_prev.wait_send()
    @pl.when(has_next)
    def _():
        to_next.wait_send()


def cross_kernel(step_bins, own_ref, next_ref, out_ref, scale_v):
    i = pl.program_id(0)
    shares, rows, segs, channels = own_ref.shape
    bins = (rows - 1) // 2
    depth = shares * segs
    row = lax.broadcasted_iota(jnp.int32, (channels, channels), 0)
    col = lax.broadcasted_iota(jnp.int32, (channels, channels), 1)

    lags = (col + row + 1) % channels

    def taken(ref, q):
        return ref[:, q].reshape(depth, channels)

    def lagged(near, far):
        chosen = jnp.where(col > row, near, far)
        return jnp.take_along_axis(chosen, lags, axis=1)

    def grams(a, b):
        return lax.dot_general(a, b, (((0,), (0,)), ((), ())), preferred_element_type=jnp.float32)

    @pl.when(i == 0)
    def _():
        here = taken(own_ref, rows - 1)
        counts = lagged(grams(here, here), grams(here, taken(next_ref, rows - 1)))
        scale_v[...] = 1.0 / jnp.maximum(counts, 1.0)

    scale = scale_v[...]
    for b in range(step_bins):
        f = i * step_bins + b
        own_re, own_im = taken(own_ref, f), taken(own_ref, bins + f)
        next_re, next_im = taken(next_ref, f), taken(next_ref, bins + f)
        left = jnp.concatenate([own_re, own_im], axis=0)
        top = jnp.concatenate([own_re, next_re, own_im, next_im], axis=1)
        low = jnp.concatenate([own_im, next_im, -own_re, -next_re], axis=1)
        gram = grams(left, jnp.concatenate([top, low], axis=0))
        cells = [gram[:, n * channels : (n + 1) * channels] for n in range(4)]
        out_ref[b, pl.ds(0, channels, 2), :] = lagged(cells[0], cells[1]) * scale
        out_ref[b, pl.ds(1, channels, 2), :] = lagged(cells[2], cells[3]) * scale


def on_device(raw_strain, fir_taps, good_mask):
    segs, channels, samples = raw_strain.shape
    fibers, shares = lax.axis_size("fiber"), lax.axis_size("seg")
    rows = 2 * NF
    per = rows // shares
    block = jax.ShapeDtypeStruct((shares, per + 1, segs, channels), jnp.bfloat16)
    vmem = pl.BlockSpec(memory_space=pltpu.VMEM)
    edges = (rows, segs * EDGE)
    own, later = pl.pallas_call(
        functools.partial(spectra_kernel, fibers, shares),
        out_shape=(block, block),
        in_specs=[
            pl.BlockSpec(memory_space=pltpu.SMEM),
            pl.BlockSpec(memory_space=pltpu.HBM),
            vmem, vmem, vmem,
        ],
        out_specs=(vmem, vmem),
        scratch_shapes=[
            pltpu.VMEM((segs // 2, 2, channels, samples), jnp.bfloat16),
            pltpu.VMEM((2, segs, EDGE, samples), jnp.bfloat16),
            pltpu.VMEM((segs // 2, rows, 2 * channels), jnp.float32),
            pltpu.VMEM(edges, jnp.float32),
            pltpu.VMEM(edges, jnp.float32),
            pltpu.VMEM(edges, jnp.float32),
            pltpu.VMEM(edges, jnp.float32),
            pltpu.VMEM((2 * channels, 2 * channels), jnp.bfloat16),
            pltpu.VMEM((segs, channels), jnp.float32),
            pltpu.VMEM((rows * segs, channels), jnp.float32),
            pltpu.VMEM(block.shape, jnp.bfloat16),
            pltpu.SemaphoreType.DMA((segs // 2,)),
            pltpu.SemaphoreType.DMA((2,)),
            pltpu.SemaphoreType.DMA((2,)),
            pltpu.SemaphoreType.DMA((2,)),
            pltpu.SemaphoreType.DMA((2 * shares,)),
            pltpu.SemaphoreType.DMA((2 * shares,)),
            pltpu.SemaphoreType.DMA((1,)),
        ],
        compiler_params=pltpu.CompilerParams(
            collective_id=0, has_side_effects=True, vmem_limit_bytes=40 * 2**20
        ),
        name="spectra",
    )(fir_taps, raw_strain, good_mask, dft_rows(samples, shares), smooth_rows(shares))

    bins = NF // shares
    step_bins = next(n for n in (4, 3, 2, 1) if bins % n == 0)
    out = pl.pallas_call(
        functools.partial(cross_kernel, step_bins),
        grid=(bins // step_bins,),
        out_shape=jax.ShapeDtypeStruct((bins, 2 * channels, LAGS), jnp.float32),
        in_specs=[vmem, vmem],
        out_specs=pl.BlockSpec((step_bins, 2 * channels, LAGS), lambda i: (i, 0, 0)),
        scratch_shapes=[pltpu.VMEM((channels, LAGS), jnp.float32)],
        compiler_params=pltpu.CompilerParams(vmem_limit_bytes=40 * 2**20),
        name="cross",
    )(own, later)
    return out.reshape(bins, channels, 2, LAGS)


def solution(mesh):
    return jax.shard_map(
        on_device,
        mesh=mesh,
        in_specs=(P("seg", "fiber", None), P(), P("seg", "fiber")),
        out_specs=P("seg", "fiber", None, None),
        check_vma=False,
    )
```

profile of v0, /device:TPU:15, one launch (start us, length us, event | category | flops | bytes accessed | tf_op | source)
XLA Modules:
  0.0 69.2 jit_solution(16165250894581587113)
XLA Ops:
  0.0 0.0 copy-start
  0.0 3.4 %copy-done = bf16[16,128,2048]{2,1,0:T(8,128)(2,1)S(1)} copy-done((bf16[16,128,2048]{2,1,0:T(8,128)(2,1)S(1)}, bf16[16,128,2048]{2,1,0:T(8,128)(2,1)}, u32[]{:S(2)}) %copy-start) | copy-done | bytes 8388632
  3.4 0.0 copy-start.1
  3.4 1.3 %copy-done.1 = bf16[288,2048]{1,0:T(8,128)(2,1)S(1)} copy-done((bf16[288,2048]{1,0:T(8,128)(2,1)S(1)}, bf16[288,2048]{1,0:T(8,128)(2,1)}, u32[]{:S(2)}) %copy-start.1) | copy-done | bytes 1179672
  4.7 0.0 copy-start.2
  4.7 0.9 %copy-done.2 = bf16[288,288]{1,0:T(8,128)(2,1)S(1)} copy-done((bf16[288,288]{1,0:T(8,128)(2,1)S(1)}, bf16[288,288]{1,0:T(8,128)(2,1)}, u32[]{:S(2)}) %copy-start.2) | copy-done | bytes 165912
  5.6 0.0 copy-start.3
  5.6 0.7 %copy-done.3 = s32[16,128]{1,0:T(8,128)S(1)} copy-done((s32[16,128]{1,0:T(8,128)S(1)}, s32[16,128]{1,0:T(8,128)}, u32[]{:S(2)}) %copy-start.3) | copy-done | bytes 8216
  6.3 0.0 copy-start.4
  6.3 0.7 copy-done.4
  6.9 54.8 %spectra.1 = (bf16[4,73,16,128]{3,2,1,0:T(8,128)(2,1)S(1)}, bf16[4,73,16,128]{3,2,1,0:T(8,128)(2,1)S(1)}) custom-call(f32[31]{0:T(128)S(1)} %copy-done.4, bf16[16,128,2048]{2,1,0:T(8,128)(2,1)S(1)} %copy-done, s32[16,128]{1,0:T(8,128)S(1)} %copy-done.3, bf16[288,2048]{1,0:T(8,128)(2,1)S(1)} %copy-done.1, bf16[288,288]{1,0:T(8,128)(2,1)S(1)} %copy-done.2), custom_call_target="tpu_custom_call" | custom-call | tf_op jit(solution)/shard_map/spectra/pallas_call | solution.py:304
  61.8 7.4 %cross.1 = f32[36,256,128]{2,1,0:T(8,128)} custom-call(bf16[4,73,16,128]{3,2,1,0:T(8,128)(2,1)S(1)} %get-tuple-element.7.own_ref, bf16[4,73,16,128]{3,2,1,0:T(8,128)(2,1)S(1)} %get-tuple-element.8.next_ref), custom_call_target="tpu_custom_call" | custom-call | tf_op jit(solution)/shard_map/cross/pallas_call | solution.py:341
Async XLA Ops:
  0.0 3.4 %copy-start = (bf16[16,128,2048]{2,1,0:T(8,128)(2,1)S(1)}, bf16[16,128,2048]{2,1,0:T(8,128)(2,1)}, u32[]{:S(2)}) copy-start(bf16[16,128,2048]{2,1,0:T(8,128)(2,1)} %raw_ref.1) | copy-start | bytes 25165828
  3.4 1.3 %copy-start.1 = (bf16[288,2048]{1,0:T(8,128)(2,1)S(1)}, bf16[288,2048]{1,0:T(8,128)(2,1)}, u32[]{:S(2)}) copy-start(bf16[288,2048]{1,0:T(8,128)(2,1)} %constant.4.clone.basis_ref) | copy-start | bytes 3538948
  4.7 0.9 %copy-start.2 = (bf16[288,288]{1,0:T(8,128)(2,1)S(1)}, bf16[288,288]{1,0:T(8,128)(2,1)}, u32[]{:S(2)}) copy-start(bf16[288,288]{1,0:T(8,128)(2,1)} %constant.5.clone.smooth_ref) | copy-start | bytes 497668
  5.6 0.7 %copy-start.3 = (s32[16,128]{1,0:T(8,128)S(1)}, s32[16,128]{1,0:T(8,128)}, u32[]{:S(2)}) copy-start(s32[16,128]{1,0:T(8,128)} %mask_ref.1) | copy-start | bytes 24580
  6.3 0.7 copy-start.4
where the time goes:
time: 69.5 us; the launch traced here: 69.2 us
  Pallas kernels  62.3 us (90%)
  local copies, waits for them, and re-layouts  6.94 us (10%)
    pallas_call x1, Pallas kernels, on_device(): pl.pallas_call(functools.partial(spectra_kernel, fibers, shares), out_sha...  54.8 us
    pallas_call x1, Pallas kernels, on_device(): pl.pallas_call(functools.partial(cross_kernel, step_bins), grid=(bins //...  7.43 us
    unnamed x10, local copies, waits for them, and re-layouts  6.94 us

commit v1 on v0

v1 whole, which is shorter than its diff:
```python
import functools
import math

import jax
import jax.numpy as jnp
import numpy as np
from jax import lax
from jax.experimental import pallas as pl
from jax.experimental.pallas import tpu as pltpu
from jax.sharding import PartitionSpec as P

NF = 144
LOW = 16
SMOOTH = 4
LAGS = 128
EDGE = 16

epsilon = 1e-06
water_share = 0.1
MESH = pl.DeviceIdType.MESH
VMEM_LIMIT = 40 * 2**20


def row_bins(shares):
    per = NF // shares
    return np.concatenate([np.tile(np.arange(k * per, (k + 1) * per), 2) for k in range(shares)])


def row_parts(shares):
    per = NF // shares
    return np.tile(np.repeat(np.arange(2), per), shares)


def dft_rows(samples, shares):
    bins, parts = row_bins(shares), row_parts(shares)
    index = ((bins[:, None] + LOW) * np.arange(samples)[None, :]) % samples
    angles = index.astype(np.float64) * (2.0 * math.pi / samples)
    return np.where(parts[:, None] == 0, np.cos(angles), -np.sin(angles)).astype(jnp.bfloat16)


def smooth_rows(shares):
    bins = row_bins(shares)
    return (np.abs(bins[:, None] - bins[None, :]) <= SMOOTH).astype(jnp.bfloat16)


def two_terms(x):
    hi = x.astype(jnp.bfloat16)
    return hi, (x - hi.astype(jnp.float32)).astype(jnp.bfloat16)


def mm(a, b):
    return jnp.dot(a, b, preferred_element_type=jnp.float32)


def mm_t(a, b):
    return lax.dot_general(a, b, (((1,), (1,)), ((), ())), preferred_element_type=jnp.float32)


def partner(seg, m):
    bit = 1
    while bit <= m:
        if m & bit:
            seg = seg + bit - 2 * bit * (seg // bit % 2)
        bit *= 2
    return seg


def spectra_kernel(
    fibers, shares, taps_ref, raw_ref, mask_ref, basis_hbm, smooth_hbm,
    own_ref, next_ref,
    raw_v, edge_v, basis_ref, smooth_ref, flag_v, spec_v, out_l, out_r, in_l, in_r, band_v, mask_v,
    white_v, send_v,
    raw_sem, edge_sem, halo_send, halo_recv, own_send, own_recv, next_send, next_recv, local_sem,
):
    fib = lax.axis_index("fiber")
    seg = lax.axis_index("seg")
    segs, channels, _ = raw_ref.shape
    rows = basis_ref.shape[0]
    per = rows // shares
    taps = taps_ref.shape[0]
    half = (taps - 1) // 2
    has_prev = fib > 0
    has_next = fib < fibers - 1
    prev = jnp.maximum(fib - 1, 0)
    following = jnp.minimum(fib + 1, fibers - 1)
    size = channels // EDGE
    chunks = segs // size
    pairs = segs // 2
    chunk_pairs = size // 2

    basis_copy = pltpu.make_async_copy(basis_hbm, basis_ref, edge_sem.at[2])
    basis_copy.start()
    edge_copies = [
        pltpu.make_async_copy(raw_ref.at[:, pl.ds(start, EDGE), :], edge_v.at[i], edge_sem.at[i])
        for i, start in enumerate((0, channels - EDGE))
    ]
    for copy in edge_copies:
        copy.start()
    mask_copy = pltpu.make_async_copy(mask_ref, flag_v, edge_sem.at[4])
    mask_copy.start()
    raw_copies = [
        pltpu.make_async_copy(raw_ref.at[pl.ds(2 * p, 2)], raw_v.at[p], raw_sem.at[p])
        for p in range(pairs)
    ]
    for copy in raw_copies:
        copy.start()
    smooth_copy = pltpu.make_async_copy(smooth_hbm, smooth_ref, edge_sem.at[3])
    smooth_copy.start()

    barrier = pltpu.get_barrier_semaphore()
    for m in range(1, shares):
        pl.semaphore_signal(
            barrier, inc=1, device_id=(fib, partner(seg, m)), device_id_type=MESH
        )
    @pl.when(has_prev)
    def _():
        pl.semaphore_signal(barrier, inc=1, device_id=(fib - 1, seg), device_id_type=MESH)
    @pl.when(has_next)
    def _():
        pl.semaphore_signal(barrier, inc=1, device_id=(fib + 1, seg), device_id_type=MESH)

    row = lax.broadcasted_iota(jnp.int32, (2 * channels, channels), 0)
    col = lax.broadcasted_iota(jnp.int32, (2 * channels, channels), 1)
    left = row - channels - EDGE
    right = row - EDGE
    place = jnp.where(row < channels, row, jnp.where(left < 0, left, right))
    place = jnp.where(row < channels + 2 * EDGE, place, 8 * channels)
    tap = place - col + half
    band = jnp.zeros((2 * channels, channels), jnp.float32)
    for j in range(taps):
        band = jnp.where(tap == j, taps_ref[j], band)
    band_hi, band_lo = two_terms(band)
    band_v[:, :channels] = band_hi
    band_v[:, channels:] = band_lo

    @pl.when(jnp.logical_not(has_prev))
    def _():
        in_l[...] = jnp.zeros_like(in_l)
    @pl.when(jnp.logical_not(has_next))
    def _():
        in_r[...] = jnp.zeros_like(in_r)
        next_ref[...] = jnp.zeros_like(next_ref)

    basis_copy.wait()
    for edge, out in ((0, out_l), (1, out_r)):
        edge_copies[edge].wait()
        ends = mm_t(basis_ref[...], edge_v[edge].reshape(segs * EDGE, -1)).astype(jnp.bfloat16)
        for c in range(chunks):
            out[c] = ends[:, c * channels : (c + 1) * channels]

    sides = (fib + fibers - 1) // fibers + (2 * fibers - 2 - fib) // fibers
    pl.semaphore_wait(barrier, shares - 1 + sides)

    to_prev = [
        pltpu.make_async_remote_copy(
            src_ref=out_l.at[c], dst_ref=in_r.at[c],
            send_sem=halo_send.at[0, c], recv_sem=halo_recv.at[0, c],
            device_id=(prev, seg), device_id_type=MESH,
        )
        for c in range(chunks)
    ]
    to_next = [
        pltpu.make_async_remote_copy(
            src_ref=out_r.at[c], dst_ref=in_l.at[c],
            send_sem=halo_send.at[1, c], recv_sem=halo_recv.at[1, c],
            device_id=(following, seg), device_id_type=MESH,
        )
        for c in range(chunks)
    ]
    for c in range(chunks):
        @pl.when(has_prev)
        def _():
            to_prev[c].start()
        @pl.when(has_next)
        def _():
            to_next[c].start()

    mask_copy.wait()
    mask_v[...] = flag_v[...].astype(jnp.float32)
    for c in range(chunks):
        flags = mask_v[c * size : (c + 1) * size, :].astype(jnp.bfloat16)
        for k in range(shares):
            send_v[k, c, per] = flags

    lane = lax.broadcasted_iota(jnp.int32, (rows, channels), 1)

    def transform(c):
        for p in range(c * chunk_pairs, (c + 1) * chunk_pairs):
            raw_copies[p].wait()
            spec_v[p] = mm_t(basis_ref[...], raw_v[p].reshape(2 * channels, -1))

    def whiten(c):
        def whiten_pair(i, carry):
            p = c * chunk_pairs + i
            lefts = in_l[c].astype(jnp.float32)
            rights = in_r[c].astype(jnp.float32)
            parts = []
            for h in range(2):
                slot = 2 * i + h
                l_roll = lax.rem(channels - slot * EDGE, channels)
                r_roll = lax.rem(channels + EDGE - slot * EDGE, channels)
                edges = jnp.where(
                    lane < EDGE, pltpu.roll(lefts, l_roll, 1), pltpu.roll(rights, r_roll, 1)
                )
                hi, lo = two_terms(spec_v[p, :, h * channels : (h + 1) * channels])
                wide = mm(jnp.concatenate([hi, edges.astype(jnp.bfloat16)], axis=1), band_v[...])
                parts.append(
                    wide[:, :channels] + wide[:, channels:] + mm(lo, band_v[:channels, :channels])
                )
            filtered = jnp.concatenate(parts, axis=1)
            power = filtered * filtered
            hi, lo = two_terms(power)
            smooth = mm(smooth_ref[...], hi) + mm(smooth_ref[...], lo)
            total = jnp.sum(power, axis=0, keepdims=True)
            level = smooth * (1.0 / (2 * SMOOTH + 1)) + (total * (water_share / NF) + epsilon)
            good = jnp.concatenate(
                [mask_v[pl.ds(2 * p, 1), :], mask_v[pl.ds(2 * p + 1, 1), :]], axis=1
            )
            white = filtered * (lax.rsqrt(level) * good)
            white_v[pl.ds(2 * i, rows, size), :] = white[:, :channels]
            white_v[pl.ds(2 * i + 1, rows, size), :] = white[:, channels:]
            return carry

        lax.fori_loop(0, chunk_pairs, whiten_pair, 0)
        for k in range(shares):
            send_v[k, c, :per] = (
                white_v[k * per * size : (k + 1) * per * size, :]
                .reshape(per, size, channels)
                .astype(jnp.bfloat16)
            )

    def to_own(c, m):
        other = partner(seg, m)
        return pltpu.make_async_remote_copy(
            src_ref=send_v.at[other, c], dst_ref=own_ref.at[seg, c],
            send_sem=own_send.at[c, m], recv_sem=own_recv.at[c, m],
            device_id=(fib, other), device_id_type=MESH,
        )

    def from_own(c, m):
        other = partner(seg, m)
        return pltpu.make_async_remote_copy(
            src_ref=send_v.at[other, c], dst_ref=own_ref.at[other, c],
            send_sem=own_send.at[c, m], recv_sem=own_recv.at[c, m],
            device_id=(fib, other), device_id_type=MESH,
        )

    def hand_on(c, m):
        source = partner(seg, m)
        block = send_v if m == 0 else own_ref
        return pltpu.make_async_remote_copy(
            src_ref=block.at[source, c], dst_ref=next_ref.at[source, c],
            send_sem=next_send.at[c, m], recv_sem=next_recv.at[c, m],
            device_id=(prev, seg), device_id_type=MESH,
        )

    def kept(c):
        return pltpu.make_async_copy(send_v.at[seg, c], own_ref.at[seg, c], local_sem.at[c])

    def give(c):
        @pl.when(has_prev)
        def _():
            hand_on(c, 0).start()
        for m in range(1, shares):
            to_own(c, m).start()
        kept(c).start()

    def relay(c, m):
        from_own(c, m).wait_recv()
        @pl.when(has_prev)
        def _():
            hand_on(c, m).start()

    smooth_copy.wait()
    waiting = []
    for c in range(chunks):
        transform(c)
        if waiting:
            relay(*waiting.pop(0))
        @pl.when(has_prev)
        def _():
            to_next[c].wait_recv()
        @pl.when(has_next)
        def _():
            to_prev[c].wait_recv()
        whiten(c)
        give(c)
        waiting += [(c, m) for m in range(1, shares)]
    for item in waiting:
        relay(*item)
    for c in range(chunks):
        kept(c).wait()
        for m in range(1, shares):
            to_own(c, m).wait_send()
    @pl.when(has_prev)
    def _():
        for c in range(chunks):
            to_prev[c].wait_send()
            for m in range(shares):
                hand_on(c, m).wait_send()
    @pl.when(has_next)
    def _():
        for c in range(chunks):
            to_next[c].wait_send()
            for m in range(shares):
                hand_on(c, m).wait_recv()


def cross_kernel(step_bins, own_ref, next_ref, out_ref, scale_v):
    i = pl.program_id(0)
    shares, chunks, rows, size, channels = own_ref.shape
    bins = (rows - 1) // 2
    depth = shares * chunks * size
    row = lax.broadcasted_iota(jnp.int32, (channels, channels), 0)
    col = lax.broadcasted_iota(jnp.int32, (channels, channels), 1)

    lags = (col + row + 1) % channels

    def taken(ref, q):
        return ref[:, :, q].reshape(depth, channels)

    def lagged(near, far):
        chosen = jnp.where(col > row, near, far)
        return jnp.take_along_axis(chosen, lags, axis=1)

    def grams(a, b):
        return lax.dot_general(a, b, (((0,), (0,)), ((), ())), preferred_element_type=jnp.float32)

    @pl.when(i == 0)
    def _():
        here = taken(own_ref, rows - 1)
        counts = lagged(grams(here, here), grams(here, taken(next_ref, rows - 1)))
        scale_v[...] = 1.0 / jnp.maximum(counts, 1.0)

    scale = scale_v[...]
    for b in range(step_bins):
        f = i * step_bins + b
        own_re, own_im = taken(own_ref, f), taken(own_ref, bins + f)
        next_re, next_im = taken(next_ref, f), taken(next_ref, bins + f)
        left = jnp.concatenate([own_re, own_im], axis=0)
        top = jnp.concatenate([own_re, next_re, own_im, next_im], axis=1)
        low = jnp.concatenate([own_im, next_im, -own_re, -next_re], axis=1)
        gram = grams(left, jnp.concatenate([top, low], axis=0))
        cells = [gram[:, n * channels : (n + 1) * channels] for n in range(4)]
        out_ref[b, pl.ds(0, channels, 2), :] = lagged(cells[0], cells[1]) * scale
        out_ref[b, pl.ds(1, channels, 2), :] = lagged(cells[2], cells[3]) * scale


def on_device(raw_strain, fir_taps, good_mask):
    segs, channels, samples = raw_strain.shape
    fibers, shares = lax.axis_size("fiber"), lax.axis_size("seg")
    rows = 2 * NF
    per = rows // shares
    size = channels // EDGE
    chunks = segs // size
    block = jax.ShapeDtypeStruct((shares, chunks, per + 1, size, channels), jnp.bfloat16)
    vmem = pl.BlockSpec(memory_space=pltpu.VMEM)
    hbm = pl.BlockSpec(memory_space=pltpu.HBM)
    edges = pltpu.VMEM((chunks, rows, size * EDGE), jnp.bfloat16)
    basis, smooth = dft_rows(samples, shares), smooth_rows(shares)
    dma = pltpu.SemaphoreType.DMA
    own, later = pl.pallas_call(
        functools.partial(spectra_kernel, fibers, shares),
        out_shape=(block, block),
        in_specs=[pl.BlockSpec(memory_space=pltpu.SMEM), hbm, hbm, hbm, hbm],
        out_specs=(vmem, vmem),
        scratch_shapes=[
            pltpu.VMEM((segs // 2, 2, channels, samples), jnp.bfloat16),
            pltpu.VMEM((2, segs, EDGE, samples), jnp.bfloat16),
            pltpu.VMEM(basis.shape, jnp.bfloat16),
            pltpu.VMEM(smooth.shape, jnp.bfloat16),
            pltpu.VMEM((segs, channels), jnp.int32),
            pltpu.VMEM((segs // 2, rows, 2 * channels), jnp.float32),
            edges, edges, edges, edges,
            pltpu.VMEM((2 * channels, 2 * channels), jnp.bfloat16),
            pltpu.VMEM((segs, channels), jnp.float32),
            pltpu.VMEM((rows * size, channels), jnp.float32),
            pltpu.VMEM(block.shape, jnp.bfloat16),
            dma((segs // 2,)),
            dma((5,)),
            dma((2, chunks)),
            dma((2, chunks)),
            dma((chunks, shares)),
            dma((chunks, shares)),
            dma((chunks, shares)),
            dma((chunks, shares)),
            dma((chunks,)),
        ],
        compiler_params=pltpu.CompilerParams(
            collective_id=0, has_side_effects=True, vmem_limit_bytes=VMEM_LIMIT
        ),
        name="spectra",
    )(
        fir_taps,
        *(
            pltpu.with_memory_space_constraint(x, pltpu.HBM)
            for x in (raw_strain, good_mask, jnp.asarray(basis), jnp.asarray(smooth))
        ),
    )

    bins = NF // shares
    step_bins = next(n for n in (4, 3, 2, 1) if bins % n == 0)
    out = pl.pallas_call(
        functools.partial(cross_kernel, step_bins),
        grid=(bins // step_bins,),
        out_shape=jax.ShapeDtypeStruct((bins, 2 * channels, LAGS), jnp.float32),
        in_specs=[vmem, vmem],
        out_specs=pl.BlockSpec((step_bins, 2 * channels, LAGS), lambda i: (i, 0, 0)),
        scratch_shapes=[pltpu.VMEM((channels, LAGS), jnp.float32)],
        compiler_params=pltpu.CompilerParams(vmem_limit_bytes=40 * 2**20),
        name="cross",
    )(own, later)
    return out.reshape(bins, channels, 2, LAGS)


def solution(mesh):
    return jax.shard_map(
        on_device,
        mesh=mesh,
        in_specs=(P("seg", "fiber", None), P(), P("seg", "fiber")),
        out_specs=P("seg", "fiber", None, None),
        check_vma=False,
    )
```

time: 69.5 us -> 51.9 us (0.75)
  the two profiles are of different devices: /device:TPU:15 before, /device:TPU:18 now
where the time goes in v1:
time: 51.9 us; the launch traced here: 51.7 us
  Pallas kernels  51.1 us (98%)
  local copies, waits for them, and re-layouts  0.65 us (1%)
    pallas_call x1, Pallas kernels, on_device(): pl.pallas_call(functools.partial(spectra_kernel, fibers, shares), out_sha...  43.6 us
    pallas_call x1, Pallas kernels, on_device(): pl.pallas_call(functools.partial(cross_kernel, step_bins), grid=(bins //...  7.43 us

profile of v1, /device:TPU:18, one launch (start us, length us, event | category | flops | bytes accessed | tf_op | source)
XLA Modules:
  0.0 51.7 jit_solution(537180206324068364)
XLA Ops:
  0.0 0.0 copy-start
  0.0 0.7 %copy-done = f32[31]{0:T(128)S(1)} copy-done((f32[31]{0:T(128)S(1)}, f32[31]{0:T(128)}, u32[]{:S(2)}) %copy-start) | copy-done | bytes 148
  0.7 43.6 %spectra.1 = (bf16[4,2,73,8,128]{4,3,2,1,0:T(8,128)(2,1)S(1)}, bf16[4,2,73,8,128]{4,3,2,1,0:T(8,128)(2,1)S(1)}) custom-call(f32[31]{0:T(128)S(1)} %copy-done, bf16[16,128,2048]{2,1,0:T(8,128)(2,1)} %raw_ref.1, s32[16,128]{1,0:T(8,128)} %mask_ref.1, bf16[288,2048]{1,0:T(8,128)(2,1)} %constant.4.clone.basis_hbm, bf16[288,288]{1,0:T(8,128)(2,1)} %constant.5.clone.smooth_hbm), custom_call_target="tpu_custom_call" | custom-call | tf_op jit(solution)/shard_map/spectra/pallas_call | solution.py:362
  44.3 7.4 %cross.1 = f32[36,256,128]{2,1,0:T(8,128)} custom-call(bf16[4,2,73,8,128]{4,3,2,1,0:T(8,128)(2,1)S(1)} %get-tuple-element.7.own_ref, bf16[4,2,73,8,128]{4,3,2,1,0:T(8,128)(2,1)S(1)} %get-tuple-element.8.next_ref), custom_call_target="tpu_custom_call" | custom-call | tf_op jit(solution)/shard_map/cross/pallas_call | solution.py:403
Async XLA Ops:
  0.0 0.7 %copy-start = (f32[31]{0:T(128)S(1)}, f32[31]{0:T(128)}, u32[]{:S(2)}) copy-start(f32[31]{0:T(128)} %taps_ref.1) | copy-start | bytes 376

commit v2 on v1

--- a/solution.py
+++ b/solution.py
@@ -56,6 +56,10 @@
     return lax.dot_general(a, b, (((1,), (1,)), ((), ())), preferred_element_type=jnp.float32)
 
 
+def turned(x, shift):
+    return pltpu.roll(x, shift, 1) if shift else x
+
+
 def partner(seg, m):
     bit = 1
     while bit <= m:
@@ -70,7 +74,7 @@
     own_ref, next_ref,
     raw_v, edge_v, basis_ref, smooth_ref, flag_v, spec_v, out_l, out_r, in_l, in_r, band_v, mask_v,
     white_v, send_v,
-    raw_sem, edge_sem, halo_send, halo_recv, own_send, own_recv, next_send, next_recv, local_sem,
+    raw_sem, edge_sem, misc_sem, halo_send, halo_recv, own_send, own_recv, next_send, next_recv, local_sem,
 ):
     fib = lax.axis_index("fiber")
     seg = lax.axis_index("seg")
@@ -88,23 +92,32 @@
     pairs = segs // 2
     chunk_pairs = size // 2
 
-    basis_copy = pltpu.make_async_copy(basis_hbm, basis_ref, edge_sem.at[2])
+    basis_copy = pltpu.make_async_copy(basis_hbm, basis_ref, misc_sem.at[0])
     basis_copy.start()
     edge_copies = [
-        pltpu.make_async_copy(raw_ref.at[:, pl.ds(start, EDGE), :], edge_v.at[i], edge_sem.at[i])
-        for i, start in enumerate((0, channels - EDGE))
+        [
+            pltpu.make_async_copy(
+                raw_ref.at[pl.ds(c * size, size), pl.ds(start, EDGE), :],
+                edge_v.at[c, i], edge_sem.at[2 * c + i],
+            )
+            for i, start in enumerate((0, channels - EDGE))
+        ]
+        for c in range(chunks)
     ]
-    for copy in edge_copies:
+    for copy in edge_copies[0]:
         copy.start()
-    mask_copy = pltpu.make_async_copy(mask_ref, flag_v, edge_sem.at[4])
+    mask_copy = pltpu.make_async_copy(mask_ref, flag_v, misc_sem.at[2])
     mask_copy.start()
     raw_copies = [
         pltpu.make_async_copy(raw_ref.at[pl.ds(2 * p, 2)], raw_v.at[p], raw_sem.at[p])
         for p in range(pairs)
     ]
-    for copy in raw_copies:
+    for p, copy in enumerate(raw_copies):
         copy.start()
-    smooth_copy = pltpu.make_async_copy(smooth_hbm, smooth_ref, edge_sem.at[3])
+        if (p + 1) % chunk_pairs == 0 and (p + 1) // chunk_pairs < chunks:
+            for edge in edge_copies[(p + 1) // chunk_pairs]:
+                edge.start()
+    smooth_copy = pltpu.make_async_copy(smooth_hbm, smooth_ref, misc_sem.at[1])
     smooth_copy.start()
 
     barrier = pltpu.get_barrier_semaphore()
@@ -141,13 +154,15 @@
         in_r[...] = jnp.zeros_like(in_r)
         next_ref[...] = jnp.zeros_like(next_ref)
 
+    def transform_edges(c):
+        for copy in edge_copies[c]:
+            copy.wait()
+        ends = mm_t(basis_ref[...], edge_v[c].reshape(2 * channels, -1)).astype(jnp.bfloat16)
+        out_l[c] = ends[:, :channels]
+        out_r[c] = ends[:, channels:]
+
     basis_copy.wait()
-    for edge, out in ((0, out_l), (1, out_r)):
-        edge_copies[edge].wait()
-        ends = mm_t(basis_ref[...], edge_v[edge].reshape(segs * EDGE, -1)).astype(jnp.bfloat16)
-        for c in range(chunks):
-            out[c] = ends[:, c * channels : (c + 1) * channels]
-
+    transform_edges(0)
     sides = (fib + fibers - 1) // fibers + (2 * fibers - 2 - fib) // fibers
     pl.semaphore_wait(barrier, shares - 1 + sides)
 
@@ -167,7 +182,7 @@
         )
         for c in range(chunks)
     ]
-    for c in range(chunks):
+    def send_edges(c):
         @pl.when(has_prev)
         def _():
             to_prev[c].start()
@@ -175,6 +190,7 @@
         def _():
             to_next[c].start()
 
+    send_edges(0)
     mask_copy.wait()
     mask_v[...] = flag_v[...].astype(jnp.float32)
     for c in range(chunks):
@@ -197,11 +213,9 @@
             parts = []
             for h in range(2):
                 slot = 2 * i + h
-                l_roll = lax.rem(channels - slot * EDGE, channels)
-                r_roll = lax.rem(channels + EDGE - slot * EDGE, channels)
-                edges = jnp.where(
-                    lane < EDGE, pltpu.roll(lefts, l_roll, 1), pltpu.roll(rights, r_roll, 1)
-                )
+                l_roll = (channels - slot * EDGE) % channels
+                r_roll = (channels + EDGE - slot * EDGE) % channels
+                edges = jnp.where(lane < EDGE, turned(lefts, l_roll), turned(rights, r_roll))
                 hi, lo = two_terms(spec_v[p, :, h * channels : (h + 1) * channels])
                 wide = mm(jnp.concatenate([hi, edges.astype(jnp.bfloat16)], axis=1), band_v[...])
                 parts.append(
@@ -209,8 +223,7 @@
                 )
             filtered = jnp.concatenate(parts, axis=1)
             power = filtered * filtered
-            hi, lo = two_terms(power)
-            smooth = mm(smooth_ref[...], hi) + mm(smooth_ref[...], lo)
+            smooth = mm(smooth_ref[...], power.astype(jnp.bfloat16))
             total = jnp.sum(power, axis=0, keepdims=True)
             level = smooth * (1.0 / (2 * SMOOTH + 1)) + (total * (water_share / NF) + epsilon)
             good = jnp.concatenate(
@@ -221,7 +234,8 @@
             white_v[pl.ds(2 * i + 1, rows, size), :] = white[:, channels:]
             return carry
 
-        lax.fori_loop(0, chunk_pairs, whiten_pair, 0)
+        for i in range(chunk_pairs):
+            whiten_pair(i, 0)
         for k in range(shares):
             send_v[k, c, :per] = (
                 white_v[k * per * size : (k + 1) * per * size, :]
@@ -275,6 +289,9 @@
     waiting = []
     for c in range(chunks):
         transform(c)
+        if c + 1 < chunks:
+            transform_edges(c + 1)
+            send_edges(c + 1)
         if waiting:
             relay(*waiting.pop(0))
         @pl.when(has_prev)
@@ -366,7 +383,7 @@
         out_specs=(vmem, vmem),
         scratch_shapes=[
             pltpu.VMEM((segs // 2, 2, channels, samples), jnp.bfloat16),
-            pltpu.VMEM((2, segs, EDGE, samples), jnp.bfloat16),
+            pltpu.VMEM((chunks, 2, size, EDGE, samples), jnp.bfloat16),
             pltpu.VMEM(basis.shape, jnp.bfloat16),
             pltpu.VMEM(smooth.shape, jnp.bfloat16),
             pltpu.VMEM((segs, channels), jnp.int32),
@@ -377,7 +394,8 @@
             pltpu.VMEM((rows * size, channels), jnp.float32),
             pltpu.VMEM(block.shape, jnp.bfloat16),
             dma((segs // 2,)),
-            dma((5,)),
+            dma((2 * chunks,)),
+            dma((3,)),
             dma((2, chunks)),
             dma((2, chunks)),
             dma((chunks, shares)),
@@ -399,7 +417,7 @@
     )
 
     bins = NF // shares
-    step_bins = next(n for n in (4, 3, 2, 1) if bins % n == 0)
+    step_bins = next(n for n in (12, 9, 6, 4, 3, 2, 1) if bins % n == 0)
     out = pl.pallas_call(
         functools.partial(cross_kernel, step_bins),
         grid=(bins // step_bins,),

time: 51.9 us -> 46.2 us (0.89)
  Pallas kernels: 51.1 us -> 44.9 us
    pallas_call x1, Pallas kernels: 43.6 us -> 39.9 us  [on_device(): pl.pallas_call(functools.partial(spectra_kernel, fibers, shares), out_sha...]
    pallas_call x1, Pallas kernels: 7.43 us -> 5.02 us  [on_device(): pl.pallas_call(functools.partial(cross_kernel, step_bins), grid=(bins //...]
where the time goes in v2:
time: 46.2 us; the launch traced here: 45.6 us
  Pallas kernels  44.9 us (97%)
  local copies, waits for them, and re-layouts  0.65 us (1%)
    pallas_call x1, Pallas kernels, on_device(): pl.pallas_call(functools.partial(spectra_kernel, fibers, shares), out_sha...  39.9 us
    pallas_call x1, Pallas kernels, on_device(): pl.pallas_call(functools.partial(cross_kernel, step_bins), grid=(bins //...  5.02 us

profile of v2, /device:TPU:18, one launch (start us, length us, event | category | flops | bytes accessed | tf_op | source)
XLA Modules:
  0.0 45.6 jit_solution(1910877512393906066)
XLA Ops:
  0.0 0.0 copy-start
  0.0 0.7 %copy-done = f32[31]{0:T(128)S(1)} copy-done((f32[31]{0:T(128)S(1)}, f32[31]{0:T(128)}, u32[]{:S(2)}) %copy-start) | copy-done | bytes 148
  0.7 39.9 %spectra.1 = (bf16[4,2,73,8,128]{4,3,2,1,0:T(8,128)(2,1)S(1)}, bf16[4,2,73,8,128]{4,3,2,1,0:T(8,128)(2,1)S(1)}) custom-call(f32[31]{0:T(128)S(1)} %copy-done, bf16[16,128,2048]{2,1,0:T(8,128)(2,1)} %raw_ref.1, s32[16,128]{1,0:T(8,128)} %mask_ref.1, bf16[288,2048]{1,0:T(8,128)(2,1)} %constant.4.clone.basis_hbm, bf16[288,288]{1,0:T(8,128)(2,1)} %constant.5.clone.smooth_hbm), custom_call_target="tpu_custom_call" | custom-call | tf_op jit(solution)/shard_map/spectra/pallas_call | solution.py:379
  40.6 5.0 %cross.1 = f32[36,256,128]{2,1,0:T(8,128)} custom-call(bf16[4,2,73,8,128]{4,3,2,1,0:T(8,128)(2,1)S(1)} %get-tuple-element.7.own_ref, bf16[4,2,73,8,128]{4,3,2,1,0:T(8,128)(2,1)S(1)} %get-tuple-element.8.next_ref), custom_call_target="tpu_custom_call" | custom-call | tf_op jit(solution)/shard_map/cross/pallas_call | solution.py:421
Async XLA Ops:
  0.0 0.7 %copy-start = (f32[31]{0:T(128)S(1)}, f32[31]{0:T(128)}, u32[]{:S(2)}) copy-start(f32[31]{0:T(128)} %taps_ref.1) | copy-start | bytes 376

commit v3 on v2

--- a/solution.py
+++ b/solution.py
@@ -69,10 +69,15 @@
     return seg
 
 
+def taken(ref, q):
+    shares, chunks, _, size, channels = ref.shape
+    return ref[:, :, q].reshape(shares * chunks * size, channels)
+
+
 def spectra_kernel(
-    fibers, shares, taps_ref, raw_ref, mask_ref, basis_hbm, smooth_hbm,
-    own_ref, next_ref,
-    raw_v, edge_v, basis_ref, smooth_ref, flag_v, spec_v, out_l, out_r, in_l, in_r, band_v, mask_v,
+    fibers, shares, taps_hbm, raw_ref, mask_ref, basis_hbm, smooth_hbm,
+    own_ref, next_ref, part_ref, turn_ref,
+    taps_ref, raw_v, edge_v, basis_ref, smooth_ref, flag_v, spec_v, out_l, out_r, in_l, in_r, band_v, mask_v,
     white_v, send_v,
     raw_sem, edge_sem, misc_sem, halo_send, halo_recv, own_send, own_recv, next_send, next_recv, local_sem,
 ):
@@ -92,6 +97,8 @@
     pairs = segs // 2
     chunk_pairs = size // 2
 
+    taps_copy = pltpu.make_async_copy(taps_hbm, taps_ref, misc_sem.at[3])
+    taps_copy.start()
     basis_copy = pltpu.make_async_copy(basis_hbm, basis_ref, misc_sem.at[0])
     basis_copy.start()
     edge_copies = [
@@ -140,6 +147,7 @@
     place = jnp.where(row < channels + 2 * EDGE, place, 8 * channels)
     tap = place - col + half
     band = jnp.zeros((2 * channels, channels), jnp.float32)
+    taps_copy.wait()
     for j in range(taps):
         band = jnp.where(tap == j, taps_ref[j], band)
     band_hi, band_lo = two_terms(band)
@@ -307,6 +315,24 @@
         relay(*item)
     for c in range(chunks):
         kept(c).wait()
+
+    bins = per // 2
+    group = next(n for n in (6, 4, 3, 2, 1) if bins % n == 0)
+
+    def own_products(i, carry):
+        for b in range(group):
+            f = i * group + b
+            re, im = taken(own_ref, f), taken(own_ref, bins + f)
+            turned_left = jnp.concatenate([re, im], axis=0).T
+            right = jnp.concatenate(
+                [jnp.concatenate([re, im], axis=1), jnp.concatenate([im, -re], axis=1)], axis=0
+            )
+            turn_ref[f] = turned_left
+            part_ref[f] = mm(turned_left, right)
+        return carry
+
+    lax.fori_loop(0, bins // group, own_products, 0)
+    for c in range(chunks):
         for m in range(1, shares):
             to_own(c, m).wait_send()
     @pl.when(has_prev)
@@ -323,18 +349,14 @@
                 hand_on(c, m).wait_recv()
 
 
-def cross_kernel(step_bins, own_ref, next_ref, out_ref, scale_v):
+def cross_kernel(step_bins, own_ref, next_ref, part_ref, turn_ref, out_ref, scale_v):
     i = pl.program_id(0)
     shares, chunks, rows, size, channels = own_ref.shape
     bins = (rows - 1) // 2
-    depth = shares * chunks * size
     row = lax.broadcasted_iota(jnp.int32, (channels, channels), 0)
     col = lax.broadcasted_iota(jnp.int32, (channels, channels), 1)
 
     lags = (col + row + 1) % channels
-
-    def taken(ref, q):
-        return ref[:, :, q].reshape(depth, channels)
 
     def lagged(near, far):
         chosen = jnp.where(col > row, near, far)
@@ -352,15 +374,14 @@
     scale = scale_v[...]
     for b in range(step_bins):
         f = i * step_bins + b
-        own_re, own_im = taken(own_ref, f), taken(own_ref, bins + f)
-        next_re, next_im = taken(next_ref, f), taken(next_ref, bins + f)
-        left = jnp.concatenate([own_re, own_im], axis=0)
-        top = jnp.concatenate([own_re, next_re, own_im, next_im], axis=1)
-        low = jnp.concatenate([own_im, next_im, -own_re, -next_re], axis=1)
-        gram = grams(left, jnp.concatenate([top, low], axis=0))
-        cells = [gram[:, n * channels : (n + 1) * channels] for n in range(4)]
-        out_ref[b, pl.ds(0, channels, 2), :] = lagged(cells[0], cells[1]) * scale
-        out_ref[b, pl.ds(1, channels, 2), :] = lagged(cells[2], cells[3]) * scale
+        re, im = taken(next_ref, f), taken(next_ref, bins + f)
+        right = jnp.concatenate(
+            [jnp.concatenate([re, im], axis=1), jnp.concatenate([im, -re], axis=1)], axis=0
+        )
+        far = mm(turn_ref[f], right)
+        for n in range(2):
+            cells = slice(n * channels, (n + 1) * channels)
+            out_ref[b, pl.ds(n, channels, 2), :] = lagged(part_ref[f, :, cells], far[:, cells]) * scale
 
 
 def on_device(raw_strain, fir_taps, good_mask):
@@ -376,12 +397,18 @@
     edges = pltpu.VMEM((chunks, rows, size * EDGE), jnp.bfloat16)
     basis, smooth = dft_rows(samples, shares), smooth_rows(shares)
     dma = pltpu.SemaphoreType.DMA
-    own, later = pl.pallas_call(
+    spectral = pl.pallas_call(
         functools.partial(spectra_kernel, fibers, shares),
-        out_shape=(block, block),
-        in_specs=[pl.BlockSpec(memory_space=pltpu.SMEM), hbm, hbm, hbm, hbm],
-        out_specs=(vmem, vmem),
+        out_shape=(
+            block,
+            block,
+            jax.ShapeDtypeStruct((per // 2, channels, 2 * channels), jnp.float32),
+            jax.ShapeDtypeStruct((per // 2, channels, 2 * shares * segs), jnp.bfloat16),
+        ),
+        in_specs=[hbm] * 5,
+        out_specs=(vmem,) * 4,
         scratch_shapes=[
+            pltpu.SMEM(fir_taps.shape, jnp.float32),
             pltpu.VMEM((segs // 2, 2, channels, samples), jnp.bfloat16),
             pltpu.VMEM((chunks, 2, size, EDGE, samples), jnp.bfloat16),
             pltpu.VMEM(basis.shape, jnp.bfloat16),
@@ -395,7 +422,7 @@
             pltpu.VMEM(block.shape, jnp.bfloat16),
             dma((segs // 2,)),
             dma((2 * chunks,)),
-            dma((3,)),
+            dma((4,)),
             dma((2, chunks)),
             dma((2, chunks)),
             dma((chunks, shares)),
@@ -409,10 +436,9 @@
         ),
         name="spectra",
     )(
-        fir_taps,
         *(
             pltpu.with_memory_space_constraint(x, pltpu.HBM)
-            for x in (raw_strain, good_mask, jnp.asarray(basis), jnp.asarray(smooth))
+            for x in (fir_taps, raw_strain, good_mask, jnp.asarray(basis), jnp.asarray(smooth))
         ),
     )
 
@@ -422,12 +448,12 @@
         functools.partial(cross_kernel, step_bins),
         grid=(bins // step_bins,),
         out_shape=jax.ShapeDtypeStruct((bins, 2 * channels, LAGS), jnp.float32),
-        in_specs=[vmem, vmem],
+        in_specs=[vmem] * 4,
         out_specs=pl.BlockSpec((step_bins, 2 * channels, LAGS), lambda i: (i, 0, 0)),
         scratch_shapes=[pltpu.VMEM((channels, LAGS), jnp.float32)],
-        compiler_params=pltpu.CompilerParams(vmem_limit_bytes=40 * 2**20),
+        compiler_params=pltpu.CompilerParams(vmem_limit_bytes=VMEM_LIMIT),
         name="cross",
-    )(own, later)
+    )(*spectral)
     return out.reshape(bins, channels, 2, LAGS)
 
 

time: 46.2 us -> 45.1 us (0.976)
  local copies, waits for them, and re-layouts: 0.65 us -> 0 us
  Pallas kernels: 44.9 us -> 44.4 us
    unnamed x2 -> x0, local copies, waits for them, and re-layouts: 0.65 us -> none
    pallas_call x1, Pallas kernels: 39.9 us -> 39.4 us  [on_device(): pl.pallas_call(functools.partial(spectra_kernel, fibers, shares), out_sha...]
where the time goes in v3:
time: 45.1 us; the launch traced here: 44.4 us
  Pallas kernels  44.4 us (98%)
    pallas_call x1, Pallas kernels, on_device(): pl.pallas_call(functools.partial(spectra_kernel, fibers, shares), out_sha...  39.4 us
    pallas_call x1, Pallas kernels, on_device(): pl.pallas_call(functools.partial(cross_kernel, step_bins), grid=(bins //...  5.04 us

profile of v3, /device:TPU:18, one launch (start us, length us, event | category | flops | bytes accessed | tf_op | source)
XLA Modules:
  0.0 44.4 jit_solution(1872533922577929855)
XLA Ops:
  0.0 39.4 %spectra.1 = (bf16[4,2,73,8,128]{4,3,2,1,0:T(8,128)(2,1)S(1)}, bf16[4,2,73,8,128]{4,3,2,1,0:T(8,128)(2,1)S(1)}, f32[36,128,256]{2,1,0:T(8,128)S(1)}, bf16[36,128,128]{2,1,0:T(8,128)(2,1)S(1)}) custom-call(f32[31]{0:T(128)} %taps_hbm.1, bf16[16,128,2048]{2,1,0:T(8,128)(2,1)} %raw_ref.1, s32[16,128]{1,0:T(8,128)} %mask_ref.1, ...), custom_call_target="tpu_custom_call" | custom-call | tf_op jit(solution)/shard_map/spectra/pallas_call | solution.py:400
  39.4 5.0 %cross.1 = f32[36,256,128]{2,1,0:T(8,128)} custom-call(bf16[4,2,73,8,128]{4,3,2,1,0:T(8,128)(2,1)S(1)} %get-tuple-element.9.own_ref, bf16[4,2,73,8,128]{4,3,2,1,0:T(8,128)(2,1)S(1)} %get-tuple-element.10.next_ref, f32[36,128,256]{2,1,0:T(8,128)S(1)} %get-tuple-element.11.part_ref, bf16[36,128,128]{2,1,0:T(8,128)(2,1)S(1)} %get-tuple-element.12.turn_ref), custom_call_target="tpu_custom_call" | custom-call | tf_op jit(solution)/shard_map/cross/pallas_call | solution.py:447
